TPU v7x, 32 devices: a whole 2x2x4 slice. The times are simulated.
32 devices in a mesh: row: 4 (over x, core), col: 8 (over z, y).
Axes of the slice: x: 2, y: 2, z: 4, core: 2. Of those that a mesh axis runs over, the one named last changes fastest.
Arguments:
- x_vals: bfloat16 [256, 32, 4096], P(('row', 'col')), may hold values from -6 to 6
- occupancy: int32 [256, 32], P(('row', 'col')), may hold values from 0 to 1, as said below
- perm: int32 [256], replicated, may hold values from 0 to 255, as said below
Outputs:
- sign_iterate_next: bfloat16 [16384, 16384], P('row', 'col')
Inputs may be any that keep to these rules, and one draw needn't show every extreme that they name: occupancy[i, s] = 1 marks block (i, (i - 16 + s) mod 256) as present; the diagonal slot s = 16 is always 1, and some row has all 32 slots 1. perm is a permutation with perm[j] = a(j mod (8)) * 32 + b(j div (8)) for permutations a and b; so the 32 band columns of any row fall exactly 4 times into each aligned run of 32 new indices, and each aligned run of 64 initial indices has exactly 16 members in each aligned run of 64 new indices.
All inputs are finite; a program needn't handle non-finite values.
Results may differ from a plain program's by a relative error of at most 0.0017.
Values may be sent and summed in bfloat16 or wider, within the bound.
A program may use at most 128 MiB of HBM per device.

v0:
```python
import math
import jax
import jax.numpy as jnp
from jax import lax
from jax.sharding import PartitionSpec as P

BLOCK_EDGE = 64


def bucket_slots(x_vals, occupancy, perm, first_row, column_processors, tile_slots):
    local_rows, band_extent = occupancy.shape
    block_count = perm.shape[0]
    panel_cols = block_count // column_processors
    row_ids = first_row + jnp.arange(local_rows, dtype=jnp.int32)
    orig_cols = (
        row_ids[:, None] - band_extent // 2 + jnp.arange(band_extent, dtype=jnp.int32)[None, :]
    ) % block_count
    new_cols = perm[orig_cols]
    panel_of = new_cols // panel_cols
    inside = new_cols % panel_cols
    in_panel = (
        (occupancy[:, :, None] == 1)
        & (panel_of[:, :, None] == jnp.arange(column_processors)[None, None, :])
    ).astype(jnp.int32)
    before = jnp.cumsum(in_panel, axis=1) - in_panel
    slot_rank = jnp.sum(before * in_panel, axis=2)
    placed = in_panel[:, :, :, None] * (
        slot_rank[:, :, None, None] == jnp.arange(tile_slots)[None, None, None, :]
    ).astype(jnp.int32)
    values = jnp.einsum(
        "kspt,ksf->pktf", placed.astype(jnp.bfloat16), x_vals, preferred_element_type=jnp.float32
    ).astype(jnp.bfloat16)
    columns = jnp.einsum("kspt,ks->pkt", placed, inside + 1) - 1
    return (values, columns)


def filtered_product(row_vals, row_cols, far_vals, far_cols, tile_cols, panel_cols):
    panel_rows, tile_slots = tile_cols.shape
    panel_count = row_vals.shape[0]
    block_area = row_vals.shape[3]
    group = math.gcd(panel_count, max(1, 16 // (tile_slots * tile_slots)))
    wanted = tile_cols >= 0

    def one_group(running, inputs):
        panel_index, piece_vals, piece_cols = inputs
        present_mask = piece_cols >= 0
        source = jnp.where(present_mask, panel_index[:, None, None] * panel_cols + piece_cols, 0)
        found_cols = far_cols[source]
        whole_rows = far_vals[source]
        chosen = jnp.zeros((group, panel_rows, tile_slots, tile_slots, block_area), far_vals.dtype)
        for slot in range(tile_slots):
            hit = (
                (found_cols[:, :, :, slot][:, :, :, None] == tile_cols[None, :, None, :])
                & present_mask[:, :, :, None]
                & wanted[None, :, None, :]
            )
            chosen = jnp.where(
                hit[:, :, :, :, None], whole_rows[:, :, :, slot][:, :, :, None, :], chosen
            )
        left_factor_blocks = piece_vals.reshape(
            group, panel_rows, tile_slots, BLOCK_EDGE, BLOCK_EDGE
        )
        right_factor_blocks = chosen.reshape(
            group, panel_rows, tile_slots, tile_slots, BLOCK_EDGE, BLOCK_EDGE
        )
        update = jnp.einsum(
            "givab,givubc->iuac",
            left_factor_blocks,
            right_factor_blocks,
            preferred_element_type=jnp.float32,
        )
        return (running + update, None)

    start = jnp.zeros((panel_rows, tile_slots, BLOCK_EDGE, BLOCK_EDGE), jnp.float32)
    panel_ids = jnp.arange(panel_count, dtype=jnp.int32).reshape(panel_count // group, group)
    grouped_vals = row_vals.reshape(panel_count // group, group, panel_rows, tile_slots, block_area)
    grouped_cols = row_cols.reshape(panel_count // group, group, panel_rows, tile_slots)
    running, _ = lax.scan(one_group, start, (panel_ids, grouped_vals, grouped_cols))
    return running.reshape(panel_rows, tile_slots, BLOCK_EDGE * BLOCK_EDGE)


def shards(x_vals, occupancy, perm):
    row_devices = lax.axis_size("row")
    column_processors = lax.axis_size("col")
    own_row = lax.axis_index("row")
    own_col = lax.axis_index("col")
    local_rows = x_vals.shape[0]
    band_extent = x_vals.shape[1]
    block_area = x_vals.shape[2]
    block_count = perm.shape[0]
    panel_rows = block_count // row_devices
    panel_cols = block_count // column_processors
    tile_slots = band_extent // column_processors
    first_row = (own_row * column_processors + own_col) * local_rows
    values, columns = bucket_slots(
        x_vals, occupancy, perm, first_row, column_processors, tile_slots
    )
    first_vals, first_cols = (
        lax.all_to_all(values, "col", split_axis=0, concat_axis=0, tiled=True),
        lax.all_to_all(
            columns.astype(jnp.bfloat16), "col", split_axis=0, concat_axis=0, tiled=True
        ),
    )
    first_vals = first_vals.reshape(panel_rows, tile_slots, block_area)
    first_cols = first_cols.astype(jnp.int32).reshape(panel_rows, tile_slots)
    group_new = lax.dynamic_slice_in_dim(perm, own_row * panel_rows, panel_rows) // panel_rows
    per_panel = panel_rows // row_devices
    heading = (group_new[:, None] == jnp.arange(row_devices)[None, :]).astype(jnp.int32)
    ahead = jnp.cumsum(heading, axis=0) - heading
    order_in = jnp.sum(ahead * heading, axis=1)
    placed = heading[:, :, None] * (
        order_in[:, None, None] == jnp.arange(per_panel)[None, None, :]
    ).astype(jnp.int32)
    send_vals = jnp.einsum(
        "gre,gtf->retf", placed.astype(jnp.bfloat16), first_vals, preferred_element_type=jnp.float32
    ).astype(jnp.bfloat16)
    send_cols = (jnp.einsum("gre,gt->ret", placed, first_cols + 1) - 1).astype(jnp.bfloat16)
    got_vals, got_cols = (
        lax.all_to_all(send_vals, "row", split_axis=0, concat_axis=0, tiled=True),
        lax.all_to_all(send_cols, "row", split_axis=0, concat_axis=0, tiled=True),
    )
    got_vals = got_vals.reshape(panel_rows, tile_slots * block_area)
    got_cols = got_cols.astype(jnp.int32).reshape(panel_rows, tile_slots)
    every_new = perm.reshape(row_devices, panel_rows)
    landing = (every_new // panel_rows == own_row).astype(jnp.int32)
    earlier = jnp.cumsum(landing, axis=1) - landing
    arrival = landing[:, :, None] * (
        earlier[:, :, None] == jnp.arange(per_panel)[None, None, :]
    ).astype(jnp.int32)
    target_row = (
        (every_new - own_row * panel_rows)[:, :, None] == jnp.arange(panel_rows)[None, None, :]
    ).astype(jnp.int32)
    selector = jnp.einsum("sge,sgl->lse", arrival, target_row).reshape(panel_rows, panel_rows)
    tile_vals = jnp.dot(
        selector.astype(jnp.bfloat16), got_vals, preferred_element_type=jnp.float32
    ).astype(jnp.bfloat16)
    tile_vals = tile_vals.reshape(panel_rows, tile_slots, block_area)
    tile_cols = jnp.dot(selector, got_cols + 1) - 1
    cols_wire = tile_cols.astype(jnp.bfloat16)
    row_vals, row_cols = (
        lax.all_gather(tile_vals[None], "col", axis=0, tiled=True),
        lax.all_gather(cols_wire[None], "col", axis=0, tiled=True),
    )
    row_cols = row_cols.astype(jnp.int32)
    far_vals, far_cols = (
        lax.all_gather(tile_vals, "row", axis=0, tiled=True),
        lax.all_gather(cols_wire, "row", axis=0, tiled=True),
    )
    far_cols = far_cols.astype(jnp.int32)
    square = filtered_product(row_vals, row_cols, far_vals, far_cols, tile_cols, panel_cols).astype(
        jnp.bfloat16
    )
    far_square = lax.all_gather(square, "row", axis=0, tiled=True)
    cube_vals = filtered_product(row_vals, row_cols, far_square, far_cols, tile_cols, panel_cols)
    stepped_matrix = (
        1.5 * tile_vals.astype(jnp.float32) - 0.5 / (BLOCK_EDGE * band_extent) * cube_vals
    )
    spread = (tile_cols[:, :, None] == jnp.arange(panel_cols)[None, None, :]).astype(jnp.float32)
    dense_tile = jnp.einsum(
        "iuj,iuac->iajc",
        spread,
        stepped_matrix.reshape(panel_rows, tile_slots, BLOCK_EDGE, BLOCK_EDGE),
    )
    return dense_tile.reshape(panel_rows * BLOCK_EDGE, panel_cols * BLOCK_EDGE).astype(jnp.bfloat16)


def solution(mesh):
    return jax.shard_map(
        shards,
        mesh=mesh,
        in_specs=(P(("row", "col"), None, None), P(("row", "col"), None), P()),
        out_specs=P("row", "col"),
        check_vma=False,
    )
```

profile of v0, /device:TPU:0, one launch (start us, length us, event | category | flops | bytes accessed | tf_op | source)
XLA Modules:
  0.0 2926.6 jit_solution(10407044865748420455)
XLA Ops:
  21.5 47.9 %all-to-all-done = bf16[8,8,4,4096]{3,2,1,0:T(4,128)(2,1)} async-done(((bf16[8,8,4,4096]{3,2,1,0:T(4,128)(2,1)}), bf16[8,8,4,4096]{3,2,1,0:T(4,128)(2,1)}, u32[]{:S(2)}, u32[]{:S(2)}) %all-to-all-start) | async-done | bytes 2097184 | tf_op jit(solution)/shard_map/all_to_all | solution.py:99
  80.5 24.8 all-to-all-done.1
  144.5 17.9 all-gather.1
  167.9 177.1 %all-gather.9.cloned.1.call-done = bf16[8,64,4,4096]{3,1,2,0:T(8,128)(2,1)} async-done(((bf16[1,64,4,4096]{3,1,2,0:T(8,128)(2,1)}), bf16[8,64,4,4096]{3,1,2,0:T(8,128)(2,1)}) %all-gather.9.cloned.1.call-update) | async-done | bytes 16777232 | tf_op jit(solution)/shard_map/all_gather | solution.py:141
  345.0 22.2 copy.185
  367.2 35.8 %all-gather.7.cloned.1.call-done = bf16[256,4,4096]{2,1,0:T(4,128)(2,1)} async-done(((bf16[64,4,4096]{2,1,0:T(4,128)(2,1)}), bf16[256,4,4096]{2,1,0:T(4,128)(2,1)}) %all-gather.7.cloned.1.call-update) | async-done | bytes 8388624 | tf_op jit(solution)/shard_map/all_gather | solution.py:146
  403.0 1186.4 %while.22 = (s32[]{:T(128)}, f32[64,4,64,64]{2,3,1,0:T(8,128)}, s32[8,1,64,4]{3,2,1,0:T(8,128)S(1)}, s32[8,1]{0,1:T(1,128)S(1)}, s32[256,4]{1,0:T(8,128)S(1)}, /...) while((s32[]{:T(128)}, f32[64,4,64,64]{2,3,1,0:T(8,128)}, ...), condition=%wide.region_6.7_spmd.clone, body=%wide.region_5.6_spmd.clone.sunk | while | flops 555760128 | bytes 94430096 | solution.py:78
  421.9 16.1 gather_fusion.1
  438.1 47.0 %slice_reduce_fusion.10 = (bf16[64,4,4096]{2,1,0:T(4,128)(2,1)}, bf16[64,4,4096]{2,1,0:T(4,128)(2,1)}, bf16[64,4,4096]{2,1,0:T(4,128)(2,1)}, bf16[64,4,4096]{2,1,0:T(4,128)(2,1)}) fusion(bf16[1,64,4,4,4096]{4,3,2,1,0:T(4,128)(2,1)} %bitcast.158), kind=kLoop, calls=%fused_computation.23.clone.1 | loop fusion | bytes 16777216 | tf_op jit(solution)/shard_map/while/body/eval_jaxpr/slice | solution.py:58
  566.9 16.1 gather_fusion.1
  583.0 47.0 %slice_reduce_fusion.10 = (bf16[64,4,4096]{2,1,0:T(4,128)(2,1)}, bf16[64,4,4096]{2,1,0:T(4,128)(2,1)}, bf16[64,4,4096]{2,1,0:T(4,128)(2,1)}, bf16[64,4,4096]{2,1,0:T(4,128)(2,1)}) fusion(bf16[1,64,4,4,4096]{4,3,2,1,0:T(4,128)(2,1)} %bitcast.158), kind=kLoop, calls=%fused_computation.23.clone.1 | loop fusion | bytes 16777216 | tf_op jit(solution)/shard_map/while/body/eval_jaxpr/slice | solution.py:58
  713.4 16.1 gather_fusion.1
  729.6 47.0 %slice_reduce_fusion.10 = (bf16[64,4,4096]{2,1,0:T(4,128)(2,1)}, bf16[64,4,4096]{2,1,0:T(4,128)(2,1)}, bf16[64,4,4096]{2,1,0:T(4,128)(2,1)}, bf16[64,4,4096]{2,1,0:T(4,128)(2,1)}) fusion(bf16[1,64,4,4,4096]{4,3,2,1,0:T(4,128)(2,1)} %bitcast.158), kind=kLoop, calls=%fused_computation.23.clone.1 | loop fusion | bytes 16777216 | tf_op jit(solution)/shard_map/while/body/eval_jaxpr/slice | solution.py:58
  860.0 16.2 gather_fusion.1
  876.1 47.0 %slice_reduce_fusion.10 = (bf16[64,4,4096]{2,1,0:T(4,128)(2,1)}, bf16[64,4,4096]{2,1,0:T(4,128)(2,1)}, bf16[64,4,4096]{2,1,0:T(4,128)(2,1)}, bf16[64,4,4096]{2,1,0:T(4,128)(2,1)}) fusion(bf16[1,64,4,4,4096]{4,3,2,1,0:T(4,128)(2,1)} %bitcast.158), kind=kLoop, calls=%fused_computation.23.clone.1 | loop fusion | bytes 16777216 | tf_op jit(solution)/shard_map/while/body/eval_jaxpr/slice | solution.py:58
  1006.5 16.1 gather_fusion.1
  1022.6 47.0 %slice_reduce_fusion.10 = (bf16[64,4,4096]{2,1,0:T(4,128)(2,1)}, bf16[64,4,4096]{2,1,0:T(4,128)(2,1)}, bf16[64,4,4096]{2,1,0:T(4,128)(2,1)}, bf16[64,4,4096]{2,1,0:T(4,128)(2,1)}) fusion(bf16[1,64,4,4,4096]{4,3,2,1,0:T(4,128)(2,1)} %bitcast.158), kind=kLoop, calls=%fused_computation.23.clone.1 | loop fusion | bytes 16777216 | tf_op jit(solution)/shard_map/while/body/eval_jaxpr/slice | solution.py:58
  1153.0 16.1 gather_fusion.1
  1169.1 47.0 %slice_reduce_fusion.10 = (bf16[64,4,4096]{2,1,0:T(4,128)(2,1)}, bf16[64,4,4096]{2,1,0:T(4,128)(2,1)}, bf16[64,4,4096]{2,1,0:T(4,128)(2,1)}, bf16[64,4,4096]{2,1,0:T(4,128)(2,1)}) fusion(bf16[1,64,4,4,4096]{4,3,2,1,0:T(4,128)(2,1)} %bitcast.158), kind=kLoop, calls=%fused_computation.23.clone.1 | loop fusion | bytes 16777216 | tf_op jit(solution)/shard_map/while/body/eval_jaxpr/slice | solution.py:58
  1299.5 16.2 gather_fusion.1
  1315.7 47.0 %slice_reduce_fusion.10 = (bf16[64,4,4096]{2,1,0:T(4,128)(2,1)}, bf16[64,4,4096]{2,1,0:T(4,128)(2,1)}, bf16[64,4,4096]{2,1,0:T(4,128)(2,1)}, bf16[64,4,4096]{2,1,0:T(4,128)(2,1)}) fusion(bf16[1,64,4,4,4096]{4,3,2,1,0:T(4,128)(2,1)} %bitcast.158), kind=kLoop, calls=%fused_computation.23.clone.1 | loop fusion | bytes 16777216 | tf_op jit(solution)/shard_map/while/body/eval_jaxpr/slice | solution.py:58
  1446.1 16.1 gather_fusion.1
  1462.2 47.0 %slice_reduce_fusion.10 = (bf16[64,4,4096]{2,1,0:T(4,128)(2,1)}, bf16[64,4,4096]{2,1,0:T(4,128)(2,1)}, bf16[64,4,4096]{2,1,0:T(4,128)(2,1)}, bf16[64,4,4096]{2,1,0:T(4,128)(2,1)}) fusion(bf16[1,64,4,4,4096]{4,3,2,1,0:T(4,128)(2,1)} %bitcast.158), kind=kLoop, calls=%fused_computation.23.clone.1 | loop fusion | bytes 16777216 | tf_op jit(solution)/shard_map/while/body/eval_jaxpr/slice | solution.py:58
  1626.1 41.7 %all-gather.11.cloned.1.call-done = bf16[256,4,4096]{2,1,0:T(4,128)(2,1)} async-done(((bf16[64,4,4096]{2,1,0:T(4,128)(2,1)}), bf16[256,4,4096]{2,1,0:T(4,128)(2,1)}) %all-gather.11.cloned.1.call-update) | async-done | bytes 8388624 | tf_op jit(solution)/shard_map/all_gather | solution.py:153
  1667.8 1172.4 %while.23 = (s32[]{:T(128)}, f32[64,4,64,64]{2,3,1,0:T(8,128)}, s32[8,1,64,4]{3,2,1,0:T(8,128)S(1)}, s32[8,1]{0,1:T(1,128)S(1)}, s32[256,4]{1,0:T(8,128)S(1)}, /...) while((s32[]{:T(128)}, f32[64,4,64,64]{2,3,1,0:T(8,128)}, ...), condition=%wide.region_8.9_spmd.clone, body=%wide.region_7.8_spmd.clone.sunk | while | flops 555760128 | bytes 94430096 | solution.py:78
  1671.5 16.1 gather_fusion.3
  1687.6 47.3 %slice_reduce_fusion.11 = (bf16[64,4,4096]{2,1,0:T(4,128)(2,1)}, bf16[64,4,4096]{2,1,0:T(4,128)(2,1)}, bf16[64,4,4096]{2,1,0:T(4,128)(2,1)}, bf16[64,4,4096]{2,1,0:T(4,128)(2,1)}) fusion(bf16[1,64,4,4,4096]{4,3,2,1,0:T(4,128)(2,1)} %bitcast.159), kind=kLoop, calls=%fused_computation.53.clone.1 | loop fusion | bytes 16777216 | tf_op jit(solution)/shard_map/while/body/eval_jaxpr/slice | solution.py:58
  1816.6 16.1 gather_fusion.3
  1832.7 47.3 %slice_reduce_fusion.11 = (bf16[64,4,4096]{2,1,0:T(4,128)(2,1)}, bf16[64,4,4096]{2,1,0:T(4,128)(2,1)}, bf16[64,4,4096]{2,1,0:T(4,128)(2,1)}, bf16[64,4,4096]{2,1,0:T(4,128)(2,1)}) fusion(bf16[1,64,4,4,4096]{4,3,2,1,0:T(4,128)(2,1)} %bitcast.159), kind=kLoop, calls=%fused_computation.53.clone.1 | loop fusion | bytes 16777216 | tf_op jit(solution)/shard_map/while/body/eval_jaxpr/slice | solution.py:58
  1944.7 15.1 bitcast_add_fusion.6
  1963.3 16.1 gather_fusion.3
  1979.4 47.3 %slice_reduce_fusion.11 = (bf16[64,4,4096]{2,1,0:T(4,128)(2,1)}, bf16[64,4,4096]{2,1,0:T(4,128)(2,1)}, bf16[64,4,4096]{2,1,0:T(4,128)(2,1)}, bf16[64,4,4096]{2,1,0:T(4,128)(2,1)}) fusion(bf16[1,64,4,4,4096]{4,3,2,1,0:T(4,128)(2,1)} %bitcast.159), kind=kLoop, calls=%fused_computation.53.clone.1 | loop fusion | bytes 16777216 | tf_op jit(solution)/shard_map/while/body/eval_jaxpr/slice | solution.py:58
  2091.4 15.1 bitcast_add_fusion.6
  2110.0 16.1 gather_fusion.3
  2126.1 47.3 %slice_reduce_fusion.11 = (bf16[64,4,4096]{2,1,0:T(4,128)(2,1)}, bf16[64,4,4096]{2,1,0:T(4,128)(2,1)}, bf16[64,4,4096]{2,1,0:T(4,128)(2,1)}, bf16[64,4,4096]{2,1,0:T(4,128)(2,1)}) fusion(bf16[1,64,4,4,4096]{4,3,2,1,0:T(4,128)(2,1)} %bitcast.159), kind=kLoop, calls=%fused_computation.53.clone.1 | loop fusion | bytes 16777216 | tf_op jit(solution)/shard_map/while/body/eval_jaxpr/slice | solution.py:58
  2256.7 16.1 gather_fusion.3
  2272.8 47.3 %slice_reduce_fusion.11 = (bf16[64,4,4096]{2,1,0:T(4,128)(2,1)}, bf16[64,4,4096]{2,1,0:T(4,128)(2,1)}, bf16[64,4,4096]{2,1,0:T(4,128)(2,1)}, bf16[64,4,4096]{2,1,0:T(4,128)(2,1)}) fusion(bf16[1,64,4,4,4096]{4,3,2,1,0:T(4,128)(2,1)} %bitcast.159), kind=kLoop, calls=%fused_computation.53.clone.1 | loop fusion | bytes 16777216 | tf_op jit(solution)/shard_map/while/body/eval_jaxpr/slice | solution.py:58
  2384.8 15.1 bitcast_add_fusion.6
  2403.4 16.1 gather_fusion.3
  2419.5 47.3 %slice_reduce_fusion.11 = (bf16[64,4,4096]{2,1,0:T(4,128)(2,1)}, bf16[64,4,4096]{2,1,0:T(4,128)(2,1)}, bf16[64,4,4096]{2,1,0:T(4,128)(2,1)}, bf16[64,4,4096]{2,1,0:T(4,128)(2,1)}) fusion(bf16[1,64,4,4,4096]{4,3,2,1,0:T(4,128)(2,1)} %bitcast.159), kind=kLoop, calls=%fused_computation.53.clone.1 | loop fusion | bytes 16777216 | tf_op jit(solution)/shard_map/while/body/eval_jaxpr/slice | solution.py:58
  2531.5 15.1 bitcast_add_fusion.6
  2550.1 16.1 gather_fusion.3
  2566.2 47.3 %slice_reduce_fusion.11 = (bf16[64,4,4096]{2,1,0:T(4,128)(2,1)}, bf16[64,4,4096]{2,1,0:T(4,128)(2,1)}, bf16[64,4,4096]{2,1,0:T(4,128)(2,1)}, bf16[64,4,4096]{2,1,0:T(4,128)(2,1)}) fusion(bf16[1,64,4,4,4096]{4,3,2,1,0:T(4,128)(2,1)} %bitcast.159), kind=kLoop, calls=%fused_computation.53.clone.1 | loop fusion | bytes 16777216 | tf_op jit(solution)/shard_map/while/body/eval_jaxpr/slice | solution.py:58
  2678.2 15.1 bitcast_add_fusion.6
  2696.8 16.1 gather_fusion.3
  2712.9 47.3 %slice_reduce_fusion.11 = (bf16[64,4,4096]{2,1,0:T(4,128)(2,1)}, bf16[64,4,4096]{2,1,0:T(4,128)(2,1)}, bf16[64,4,4096]{2,1,0:T(4,128)(2,1)}, bf16[64,4,4096]{2,1,0:T(4,128)(2,1)}) fusion(bf16[1,64,4,4,4096]{4,3,2,1,0:T(4,128)(2,1)} %bitcast.159), kind=kLoop, calls=%fused_computation.53.clone.1 | loop fusion | bytes 16777216 | tf_op jit(solution)/shard_map/while/body/eval_jaxpr/slice | solution.py:58
  2857.6 16.1 convert_bitcast_fusion
  2873.7 46.0 %convert_element_type.138 = bf16[4096,2048]{1,0:T(8,128)(2,1)} reshape(bf16[64,64,32,64]{3,2,1,0:T(8,128)(2,1)} %convert_bitcast_fusion) | data formatting | bytes 33554432 | tf_op jit(solution)/shard_map/convert_element_type | solution.py:164
  (493 shorter events, 1379.0 us)
Async XLA Ops:
  6.5 3.6 copy-start
  6.5 2.3 copy-start.3
  10.8 10.3 copy-start.2
  13.8 55.6 %all-to-all-start = ((bf16[8,8,4,4096]{3,2,1,0:T(4,128)(2,1)}), bf16[8,8,4,4096]{3,2,1,0:T(4,128)(2,1)}, u32[]{:S(2)}, u32[]{:S(2)}) async-start(bf16[8,8,4,4096]{3,2,1,0:T(4,128)(2,1)} %copy.175), calls=%async_computation | async-start | bytes 4194304 | tf_op jit(solution)/shard_map/all_to_all | solution.py:99
  75.2 30.2 %all-to-all-start.1 = ((bf16[4,16,4,4096]{3,1,2,0:T(8,128)(2,1)}), bf16[4,16,4,4096]{3,1,2,0:T(8,128)(2,1)}, u32[]{:S(2)}, u32[]{:S(2)}) async-start(bf16[4,16,4,4096]{3,1,2,0:T(8,128)(2,1)} %convolution_convert_fusion.1), calls=%async_computation.1 | async-start | bytes 4194304 | tf_op jit(solution)/shard_map/all_to_all | solution.py:119
  79.6 265.4 %all-gather.9.cloned.1.call-start = ((), (), s32[]{:S(2)}) async-start(), calls=%async_computation.5 | async-start | bytes 18874368 | tf_op jit(solution)/shard_map/all_gather | solution.py:141
  119.4 283.6 %all-gather.7.cloned.1.call-start = ((), (), s32[]{:S(2)}) async-start(), calls=%async_computation.4 | async-start | bytes 10485760 | tf_op jit(solution)/shard_map/all_gather | solution.py:146
  137.2 7.0 all-to-all-start.3
  140.5 1527.3 %all-gather.11.cloned.1.call-start = ((), (), s32[]{:S(2)}) async-start(), calls=%async_computation.6 | async-start | bytes 10485760 | tf_op jit(solution)/shard_map/all_gather | solution.py:153
  2873.7 46.0 %copy-start.1 = (bf16[8,32,4096]{2,1,0:T(8,128)(2,1)S(1)}, bf16[8,32,4096]{2,1,0:T(8,128)(2,1)}, u32[]{:S(2)}) copy-start(bf16[8,32,4096]{2,1,0:T(8,128)(2,1)} %param.7) | copy-start | bytes 6291460
Sparse Core Ops, SparseCore 0:
  119.5 225.4 all-gather.8
  346.6 56.4 all-gather.6
  1609.5 58.2 all-gather.10
where the time goes:
time: 2960 us; the launch traced here: 2930 us
  local copies, waits for them, and re-layouts  2210 us (75%)
  waiting for transfers between devices  331 us (11%)
  matrix products  268 us (9%)
  other arithmetic  42.8 us (1%)
  blocking collectives  33.6 us (1%)
    broadcast_in_dim x128, local copies, waits for them, and re-layouts, one_group(): jnp.where(hit[:, :, :, :, None], whole_rows[:, :, :, slot][:, :, :, None,...  853 us
    slice x16, local copies, waits for them, and re-layouts, one_group(): whole_rows[:, :, :, slot][:, :, :, None, :]  755 us
    gather x16, local copies, waits for them, and re-layouts, one_group(): whole_rows = far_vals[source]  258 us
    dot_general x16, matrix products, one_group(): jnp.einsum('givab,givubc->iuac', left_factor_blocks, right_factor_blocks,...  238 us
    all_gather x1, waiting for transfers between devices, shards(): lax.all_gather(tile_vals[None], 'col', axis=0, tiled=True)  177 us
    another operation x16, local copies, waits for them, and re-layouts  112 us
    dynamic_slice x16, local copies, waits for them, and re-layouts, filtered_product(): lax.scan(one_group, start, (panel_ids, grouped_vals, grouped_cols))  72.1 us
  transfers between devices with their start and end apart: 6, of which 6 were waited for; matrix products, arithmetic and copies ran while one was open for 2% of the time, Pallas kernels for 0%

commit v1 on v0

--- a/solution.py
+++ b/solution.py
@@ -138,7 +138,9 @@
     tile_cols = jnp.dot(selector, got_cols + 1) - 1
     cols_wire = tile_cols.astype(jnp.bfloat16)
     row_vals, row_cols = (
-        lax.all_gather(tile_vals[None], "col", axis=0, tiled=True),
+        jnp.concatenate(
+            lax.all_to_all(jnp.stack([tile_vals[None]] * lax.axis_size("col")), "col", 0, 0), axis=0
+        ),
         lax.all_gather(cols_wire[None], "col", axis=0, tiled=True),
     )
     row_cols = row_cols.astype(jnp.int32)

time: 2960 us -> 3070 us (1.037)
  blocking collectives: 33.6 us -> 291 us
  waiting for transfers between devices: 331 us -> 196 us
    all_gather x1, blocking collectives: 17.9 us -> 285 us  [shards(): lax.all_gather(cols_wire[None], 'col', axis=0, tiled=True)]
    all_gather x1 -> x0, waiting for transfers between devices: 177 us -> none  [shards(): lax.all_gather(tile_vals[None], 'col', axis=0, tiled=True)]
    all_to_all x0 -> x2, waiting for transfers between devices: none -> 72.5 us  [the longest x1 71.7 us: shards(): lax.all_to_all(jnp.stack([tile_vals[None]] * lax.axis_size('col')), 'col'...]
    all_gather x1, waiting for transfers between devices: 35.8 us -> 0.02 us  [shards(): lax.all_gather(tile_vals, 'row', axis=0, tiled=True)]
  transfers between devices with their start and end apart: 6 -> 7, of which waited for: 6 -> 5; matrix products, arithmetic and copies ran while one was open for 2% -> 1% of each run, Pallas kernels for 0% -> 0%
where the time goes in v1:
time: 3070 us; the launch traced here: 3040 us
  local copies, waits for them, and re-layouts  2180 us (71%)
  blocking collectives  291 us (9%)
  matrix products  268 us (9%)
  waiting for transfers between devices  196 us (6%)
  other arithmetic  43.7 us (1%)
    broadcast_in_dim x128, local copies, waits for them, and re-layouts, one_group(): jnp.where(hit[:, :, :, :, None], whole_rows[:, :, :, slot][:, :, :, None,...  853 us
    slice x16, local copies, waits for them, and re-layouts, one_group(): whole_rows[:, :, :, slot][:, :, :, None, :]  753 us
    all_gather x1, blocking collectives, shards(): lax.all_gather(cols_wire[None], 'col', axis=0, tiled=True)  285 us
    gather x16, local copies, waits for them, and re-layouts, one_group(): whole_rows = far_vals[source]  258 us
    dot_general x16, matrix products, one_group(): jnp.einsum('givab,givubc->iuac', left_factor_blocks, right_factor_blocks,...  238 us
    another operation x16, local copies, waits for them, and re-layouts  112 us
    all_to_all x1, waiting for transfers between devices, shards(): lax.all_to_all(jnp.stack([tile_vals[None]] * lax.axis_size('col')), 'col'...  71.7 us
    dynamic_slice x16, local copies, waits for them, and re-layouts, filtered_product(): lax.scan(one_group, start, (panel_ids, grouped_vals, grouped_cols))  71.6 us
  transfers between devices with their start and end apart: 7, of which 5 were waited for; matrix products, arithmetic and copies ran while one was open for 1% of the time, Pallas kernels for 0%

profile of v1, /device:TPU:0, one launch (start us, length us, event | category | flops | bytes accessed | tf_op | source)
XLA Modules:
  0.0 3037.8 jit_solution(11395000899656922657)
XLA Ops:
  25.2 44.3 %all-to-all-done = bf16[8,8,4,4096]{3,2,1,0:T(4,128)(2,1)} async-done(((bf16[8,8,4,4096]{3,2,1,0:T(4,128)(2,1)}), bf16[8,8,4,4096]{3,2,1,0:T(4,128)(2,1)}, u32[]{:S(2)}, u32[]{:S(2)}) %all-to-all-start) | async-done | bytes 2097184 | tf_op jit(solution)/shard_map/all_to_all | solution.py:99
  85.9 23.9 all-to-all-done.1
  140.1 285.5 %all-gather.1 = bf16[8,64,4]{1,2,0:T(4,128)(2,1)S(1)} all-gather(bf16[1,64,4]{1,2,0:T(4,128)(2,1)S(1)} %convert_bitcast_fusion.1), channel_id=2, replica_groups=mesh['row'=4,'col'=8] {'col'}, dimensions={0}, use_global_device_ids=true | all-gather | bytes 4608 | tf_op jit(solution)/shard_map/all_gather | solution.py:144
  431.1 71.7 %all-to-all-done.4 = bf16[8,1,64,4,4096]{4,3,2,1,0:T(4,128)(2,1)} async-done(((bf16[8,1,64,4,4096]{4,3,2,1,0:T(4,128)(2,1)}), bf16[8,1,64,4,4096]{4,3,2,1,0:T(4,128)(2,1)}, u32[]{:S(2)}, u32[]{:S(2)}) %all-to-all-start.4) | async-done | bytes 16777248 | tf_op jit(solution)/shard_map/all_to_all | solution.py:142
  502.8 1186.1 %while.22 = (s32[]{:T(128)}, f32[64,4,64,64]{2,3,1,0:T(8,128)}, s32[8,1,64,4]{3,2,1,0:T(8,128)S(1)}, s32[8,1]{0,1:T(1,128)S(1)}, s32[256,4]{1,0:T(8,128)S(1)}, /...) while((s32[]{:T(128)}, f32[64,4,64,64]{2,3,1,0:T(8,128)}, ...), condition=%wide.region_6.7_spmd.clone, body=%wide.region_5.6_spmd.clone.sunk | while | flops 555760128 | bytes 94430096 | solution.py:78
  521.7 16.1 gather_fusion.1
  537.8 47.0 %slice_reduce_fusion.10 = (bf16[64,4,4096]{2,1,0:T(4,128)(2,1)}, bf16[64,4,4096]{2,1,0:T(4,128)(2,1)}, bf16[64,4,4096]{2,1,0:T(4,128)(2,1)}, bf16[64,4,4096]{2,1,0:T(4,128)(2,1)}) fusion(bf16[1,64,4,4,4096]{4,3,2,1,0:T(4,128)(2,1)} %bitcast.157), kind=kLoop, calls=%fused_computation.23.clone.1 | loop fusion | bytes 16777216 | tf_op jit(solution)/shard_map/while/body/eval_jaxpr/slice | solution.py:58
  666.6 16.1 gather_fusion.1
  682.7 47.0 %slice_reduce_fusion.10 = (bf16[64,4,4096]{2,1,0:T(4,128)(2,1)}, bf16[64,4,4096]{2,1,0:T(4,128)(2,1)}, bf16[64,4,4096]{2,1,0:T(4,128)(2,1)}, bf16[64,4,4096]{2,1,0:T(4,128)(2,1)}) fusion(bf16[1,64,4,4,4096]{4,3,2,1,0:T(4,128)(2,1)} %bitcast.157), kind=kLoop, calls=%fused_computation.23.clone.1 | loop fusion | bytes 16777216 | tf_op jit(solution)/shard_map/while/body/eval_jaxpr/slice | solution.py:58
  813.1 16.1 gather_fusion.1
  829.2 47.0 %slice_reduce_fusion.10 = (bf16[64,4,4096]{2,1,0:T(4,128)(2,1)}, bf16[64,4,4096]{2,1,0:T(4,128)(2,1)}, bf16[64,4,4096]{2,1,0:T(4,128)(2,1)}, bf16[64,4,4096]{2,1,0:T(4,128)(2,1)}) fusion(bf16[1,64,4,4,4096]{4,3,2,1,0:T(4,128)(2,1)} %bitcast.157), kind=kLoop, calls=%fused_computation.23.clone.1 | loop fusion | bytes 16777216 | tf_op jit(solution)/shard_map/while/body/eval_jaxpr/slice | solution.py:58
  959.6 16.1 gather_fusion.1
  975.7 47.0 %slice_reduce_fusion.10 = (bf16[64,4,4096]{2,1,0:T(4,128)(2,1)}, bf16[64,4,4096]{2,1,0:T(4,128)(2,1)}, bf16[64,4,4096]{2,1,0:T(4,128)(2,1)}, bf16[64,4,4096]{2,1,0:T(4,128)(2,1)}) fusion(bf16[1,64,4,4,4096]{4,3,2,1,0:T(4,128)(2,1)} %bitcast.157), kind=kLoop, calls=%fused_computation.23.clone.1 | loop fusion | bytes 16777216 | tf_op jit(solution)/shard_map/while/body/eval_jaxpr/slice | solution.py:58
  1106.1 16.1 gather_fusion.1
  1122.2 47.0 %slice_reduce_fusion.10 = (bf16[64,4,4096]{2,1,0:T(4,128)(2,1)}, bf16[64,4,4096]{2,1,0:T(4,128)(2,1)}, bf16[64,4,4096]{2,1,0:T(4,128)(2,1)}, bf16[64,4,4096]{2,1,0:T(4,128)(2,1)}) fusion(bf16[1,64,4,4,4096]{4,3,2,1,0:T(4,128)(2,1)} %bitcast.157), kind=kLoop, calls=%fused_computation.23.clone.1 | loop fusion | bytes 16777216 | tf_op jit(solution)/shard_map/while/body/eval_jaxpr/slice | solution.py:58
  1252.5 16.1 gather_fusion.1
  1268.6 47.0 %slice_reduce_fusion.10 = (bf16[64,4,4096]{2,1,0:T(4,128)(2,1)}, bf16[64,4,4096]{2,1,0:T(4,128)(2,1)}, bf16[64,4,4096]{2,1,0:T(4,128)(2,1)}, bf16[64,4,4096]{2,1,0:T(4,128)(2,1)}) fusion(bf16[1,64,4,4,4096]{4,3,2,1,0:T(4,128)(2,1)} %bitcast.157), kind=kLoop, calls=%fused_computation.23.clone.1 | loop fusion | bytes 16777216 | tf_op jit(solution)/shard_map/while/body/eval_jaxpr/slice | solution.py:58
  1399.0 16.1 gather_fusion.1
  1415.1 47.0 %slice_reduce_fusion.10 = (bf16[64,4,4096]{2,1,0:T(4,128)(2,1)}, bf16[64,4,4096]{2,1,0:T(4,128)(2,1)}, bf16[64,4,4096]{2,1,0:T(4,128)(2,1)}, bf16[64,4,4096]{2,1,0:T(4,128)(2,1)}) fusion(bf16[1,64,4,4,4096]{4,3,2,1,0:T(4,128)(2,1)} %bitcast.157), kind=kLoop, calls=%fused_computation.23.clone.1 | loop fusion | bytes 16777216 | tf_op jit(solution)/shard_map/while/body/eval_jaxpr/slice | solution.py:58
  1545.5 16.1 gather_fusion.1
  1561.6 47.0 %slice_reduce_fusion.10 = (bf16[64,4,4096]{2,1,0:T(4,128)(2,1)}, bf16[64,4,4096]{2,1,0:T(4,128)(2,1)}, bf16[64,4,4096]{2,1,0:T(4,128)(2,1)}, bf16[64,4,4096]{2,1,0:T(4,128)(2,1)}) fusion(bf16[1,64,4,4,4096]{4,3,2,1,0:T(4,128)(2,1)} %bitcast.157), kind=kLoop, calls=%fused_computation.23.clone.1 | loop fusion | bytes 16777216 | tf_op jit(solution)/shard_map/while/body/eval_jaxpr/slice | solution.py:58
  1673.4 15.1 bitcast_add_fusion.5
  1725.2 55.1 %all-gather.8.cloned.1.call-done = bf16[256,4,4096]{2,1,0:T(4,128)(2,1)} async-done(((bf16[64,4,4096]{2,1,0:T(4,128)(2,1)}), bf16[256,4,4096]{2,1,0:T(4,128)(2,1)}) %all-gather.8.cloned.1.call-update) | async-done | bytes 8388624 | tf_op jit(solution)/shard_map/all_gather | solution.py:155
  1780.3 1170.7 %while.23 = (s32[]{:T(128)}, f32[64,4,64,64]{2,3,1,0:T(8,128)}, s32[8,1,64,4]{3,2,1,0:T(8,128)S(1)}, s32[8,1]{0,1:T(1,128)S(1)}, s32[256,4]{1,0:T(8,128)S(1)}, /...) while((s32[]{:T(128)}, f32[64,4,64,64]{2,3,1,0:T(8,128)}, ...), condition=%wide.region_8.9_spmd.clone, body=%wide.region_7.8_spmd.clone.sunk | while | flops 555760128 | bytes 94430096 | solution.py:78
  1784.0 16.1 gather_fusion.3
  1800.1 47.0 %slice_reduce_fusion.11 = (bf16[64,4,4096]{2,1,0:T(4,128)(2,1)}, bf16[64,4,4096]{2,1,0:T(4,128)(2,1)}, bf16[64,4,4096]{2,1,0:T(4,128)(2,1)}, bf16[64,4,4096]{2,1,0:T(4,128)(2,1)}) fusion(bf16[1,64,4,4,4096]{4,3,2,1,0:T(4,128)(2,1)} %bitcast.158), kind=kLoop, calls=%fused_computation.53.clone.1 | loop fusion | bytes 16777216 | tf_op jit(solution)/shard_map/while/body/eval_jaxpr/slice | solution.py:58
  1928.9 16.1 gather_fusion.3
  1945.0 47.0 %slice_reduce_fusion.11 = (bf16[64,4,4096]{2,1,0:T(4,128)(2,1)}, bf16[64,4,4096]{2,1,0:T(4,128)(2,1)}, bf16[64,4,4096]{2,1,0:T(4,128)(2,1)}, bf16[64,4,4096]{2,1,0:T(4,128)(2,1)}) fusion(bf16[1,64,4,4,4096]{4,3,2,1,0:T(4,128)(2,1)} %bitcast.158), kind=kLoop, calls=%fused_computation.53.clone.1 | loop fusion | bytes 16777216 | tf_op jit(solution)/shard_map/while/body/eval_jaxpr/slice | solution.py:58
  2056.8 15.1 bitcast_add_fusion.6
  2075.4 16.1 gather_fusion.3
  2091.5 47.0 %slice_reduce_fusion.11 = (bf16[64,4,4096]{2,1,0:T(4,128)(2,1)}, bf16[64,4,4096]{2,1,0:T(4,128)(2,1)}, bf16[64,4,4096]{2,1,0:T(4,128)(2,1)}, bf16[64,4,4096]{2,1,0:T(4,128)(2,1)}) fusion(bf16[1,64,4,4,4096]{4,3,2,1,0:T(4,128)(2,1)} %bitcast.158), kind=kLoop, calls=%fused_computation.53.clone.1 | loop fusion | bytes 16777216 | tf_op jit(solution)/shard_map/while/body/eval_jaxpr/slice | solution.py:58
  2203.3 15.1 bitcast_add_fusion.6
  2221.9 16.1 gather_fusion.3
  2238.1 47.0 %slice_reduce_fusion.11 = (bf16[64,4,4096]{2,1,0:T(4,128)(2,1)}, bf16[64,4,4096]{2,1,0:T(4,128)(2,1)}, bf16[64,4,4096]{2,1,0:T(4,128)(2,1)}, bf16[64,4,4096]{2,1,0:T(4,128)(2,1)}) fusion(bf16[1,64,4,4,4096]{4,3,2,1,0:T(4,128)(2,1)} %bitcast.158), kind=kLoop, calls=%fused_computation.53.clone.1 | loop fusion | bytes 16777216 | tf_op jit(solution)/shard_map/while/body/eval_jaxpr/slice | solution.py:58
  2349.9 15.1 bitcast_add_fusion.6
  2368.4 16.1 gather_fusion.3
  2384.5 47.0 %slice_reduce_fusion.11 = (bf16[64,4,4096]{2,1,0:T(4,128)(2,1)}, bf16[64,4,4096]{2,1,0:T(4,128)(2,1)}, bf16[64,4,4096]{2,1,0:T(4,128)(2,1)}, bf16[64,4,4096]{2,1,0:T(4,128)(2,1)}) fusion(bf16[1,64,4,4,4096]{4,3,2,1,0:T(4,128)(2,1)} %bitcast.158), kind=kLoop, calls=%fused_computation.53.clone.1 | loop fusion | bytes 16777216 | tf_op jit(solution)/shard_map/while/body/eval_jaxpr/slice | solution.py:58
  2496.3 15.1 bitcast_add_fusion.6
  2514.9 16.1 gather_fusion.3
  2531.0 47.0 %slice_reduce_fusion.11 = (bf16[64,4,4096]{2,1,0:T(4,128)(2,1)}, bf16[64,4,4096]{2,1,0:T(4,128)(2,1)}, bf16[64,4,4096]{2,1,0:T(4,128)(2,1)}, bf16[64,4,4096]{2,1,0:T(4,128)(2,1)}) fusion(bf16[1,64,4,4,4096]{4,3,2,1,0:T(4,128)(2,1)} %bitcast.158), kind=kLoop, calls=%fused_computation.53.clone.1 | loop fusion | bytes 16777216 | tf_op jit(solution)/shard_map/while/body/eval_jaxpr/slice | solution.py:58
  2642.8 15.1 bitcast_add_fusion.6
  2661.4 16.1 gather_fusion.3
  2677.5 47.0 %slice_reduce_fusion.11 = (bf16[64,4,4096]{2,1,0:T(4,128)(2,1)}, bf16[64,4,4096]{2,1,0:T(4,128)(2,1)}, bf16[64,4,4096]{2,1,0:T(4,128)(2,1)}, bf16[64,4,4096]{2,1,0:T(4,128)(2,1)}) fusion(bf16[1,64,4,4,4096]{4,3,2,1,0:T(4,128)(2,1)} %bitcast.158), kind=kLoop, calls=%fused_computation.53.clone.1 | loop fusion | bytes 16777216 | tf_op jit(solution)/shard_map/while/body/eval_jaxpr/slice | solution.py:58
  2789.3 15.1 bitcast_add_fusion.6
  2807.9 16.1 gather_fusion.3
  2824.0 47.0 %slice_reduce_fusion.11 = (bf16[64,4,4096]{2,1,0:T(4,128)(2,1)}, bf16[64,4,4096]{2,1,0:T(4,128)(2,1)}, bf16[64,4,4096]{2,1,0:T(4,128)(2,1)}, bf16[64,4,4096]{2,1,0:T(4,128)(2,1)}) fusion(bf16[1,64,4,4,4096]{4,3,2,1,0:T(4,128)(2,1)} %bitcast.158), kind=kLoop, calls=%fused_computation.53.clone.1 | loop fusion | bytes 16777216 | tf_op jit(solution)/shard_map/while/body/eval_jaxpr/slice | solution.py:58
  2968.5 16.1 convert_bitcast_fusion
  2984.5 46.0 %convert_element_type.138 = bf16[4096,2048]{1,0:T(8,128)(2,1)} reshape(bf16[64,64,32,64]{3,2,1,0:T(8,128)(2,1)} %convert_bitcast_fusion) | data formatting | bytes 33554432 | tf_op jit(solution)/shard_map/convert_element_type | solution.py:166
  (493 shorter events, 1348.7 us)
Async XLA Ops:
  6.5 3.6 copy-start
  6.5 2.3 copy-start.4
  10.8 10.3 copy-start.2
  13.8 55.7 %all-to-all-start = ((bf16[8,8,4,4096]{3,2,1,0:T(4,128)(2,1)}), bf16[8,8,4,4096]{3,2,1,0:T(4,128)(2,1)}, u32[]{:S(2)}, u32[]{:S(2)}) async-start(bf16[8,8,4,4096]{3,2,1,0:T(4,128)(2,1)} %copy.172), calls=%async_computation | async-start | bytes 4194304 | tf_op jit(solution)/shard_map/all_to_all | solution.py:99
  69.4 10.2 all-to-all-start.2
  79.6 30.2 all-to-all-start.1
  109.8 14.6 all-to-all-start.3
  124.4 8.8 copy-start.3
  133.2 369.5 %all-to-all-start.4 = ((bf16[8,1,64,4,4096]{4,3,2,1,0:T(4,128)(2,1)}), bf16[8,1,64,4,4096]{4,3,2,1,0:T(4,128)(2,1)}, u32[]{:S(2)}, u32[]{:S(2)}) async-start(bf16[8,1,64,4,4096]{4,3,2,1,0:T(4,128)(2,1)} %stack.3), calls=%async_computation.4 | async-start | bytes 33554432 | tf_op jit(solution)/shard_map/all_to_all | solution.py:142
  139.0 292.1 %all-gather.6.cloned.1.call-start = ((), (), s32[]{:S(2)}) async-start(), calls=%async_computation.5 | async-start | bytes 10485760 | tf_op jit(solution)/shard_map/all_gather | solution.py:148
  139.7 1640.6 %all-gather.8.cloned.1.call-start = ((), (), s32[]{:S(2)}) async-start(), calls=%async_computation.6 | async-start | bytes 10485760 | tf_op jit(solution)/shard_map/all_gather | solution.py:155
  2984.5 46.0 %copy-start.1 = (bf16[8,32,4096]{2,1,0:T(8,128)(2,1)S(1)}, bf16[8,32,4096]{2,1,0:T(8,128)(2,1)}, u32[]{:S(2)}) copy-start(bf16[8,32,4096]{2,1,0:T(8,128)(2,1)} %param.7) | copy-start | bytes 6291460
Sparse Core Ops, SparseCore 0:
  141.3 60.0 all-gather.5
  1709.0 71.2 all-gather.7
